TPU v7x, 32 devices: a whole 2x2x4 slice. The times are simulated.
32 devices in a mesh: blk: 8 (over y, x, core), feat: 4 (over z).
Axes of the slice: x: 2, y: 2, z: 4, core: 2. Of those that a mesh axis runs over, the one named last changes fastest.
Arguments:
- features: bfloat16 [128, 8192], P('feat', 'blk'), may hold values from -6 to 6
- weight_in: bfloat16 [128, 256], replicated, may hold values from -0.5 to 0.5
- weight_mid: bfloat16 [256, 256], replicated, may hold values from -0.375 to 0.375
- weight_out: bfloat16 [256, 172], replicated, may hold values from -0.375 to 0.375
- block_values: bfloat16 [8, 8, 16, 128, 128], P('blk'), may hold values from -0.25 to 0.25
- block_dst: int32 [8, 8, 16], P('blk'), may hold values from 0 to 7
- block_src: int32 [8, 8, 16], P('blk'), may hold values from 0 to 7
- block_count: int32 [8, 8], P('blk'), may hold values from 4 to 16, as said below
- labels: int32 [8192], P('blk'), may hold values from 0 to 171
- train_mask: int32 [8192], P('blk'), may hold values from 0 to 1
Outputs:
- loss: float32 [], replicated
- grad_in: float32 [128, 256], P('feat')
- grad_mid: float32 [256, 256], P('feat')
- grad_out: float32 [256, 172], P('feat')
Inputs may be any that keep to these rules, and one draw needn't show every extreme that they name: block_count[b, p] is the number of live slots of the blocks of panel b's rows that read panel p's nodes; block_count[b, b] = 16. Entries of block_dst, block_src and block_values at slots at or past block_count are unused.
All inputs are finite; a program needn't handle non-finite values.
Results may differ from a plain program's by a relative error of at most 0.017.
Values may be sent and summed in bfloat16 or wider, within the bound.
A program may use at most 64 MiB of HBM per device.

v0:
```python
import jax
import jax.numpy as jnp
from jax import lax
from jax.sharding import PartitionSpec as P


def elu(values):
    return jnp.where(values > 0, values, jnp.expm1(values))


def elu_slope(values):
    return jnp.where(values > 0, 1.0, jnp.exp(values))


def panel_folder(values, targets, sources, live_count, breadth, row_blocks, block_size):
    panel_rows = row_blocks * block_size
    slot_index = jnp.arange(values.shape[2], dtype=jnp.int32)

    def folding(running, portion, offset):
        several = portion.shape[1] // panel_rows

        def folding_one_panel(turn_index, accumulated):
            window = lax.dynamic_slice_in_dim(portion, turn_index * panel_rows, panel_rows, 1)
            window = window.reshape(breadth, row_blocks, block_size)
            chosen = jnp.take(window, sources[0, turn_index], axis=1)
            product = jnp.einsum(
                "fsj,sij->fsi", chosen, values[0, turn_index], preferred_element_type=jnp.float32
            )
            live_slots = (slot_index < live_count[0, turn_index]).astype(jnp.float32)
            return accumulated.at[:, targets[0, turn_index]].add(
                product * live_slots[None, :, None]
            )

        return lax.fori_loop(0, several, folding_one_panel, running)

    return folding


def hidden_aggregate(table, values, targets, sources, live_count):
    breadth, panel_rows = table.shape
    block_size = values.shape[-1]
    row_blocks = panel_rows // block_size
    folding = panel_folder(values, targets, sources, live_count, breadth, row_blocks, block_size)
    initial = jnp.zeros((breadth, row_blocks, block_size), jnp.float32)
    summed = folding(initial, lax.all_gather(table, "blk", axis=1, tiled=True), jnp.int32(0))
    return summed.reshape(breadth, panel_rows).astype(jnp.bfloat16)


def spread_back(grads, values, targets, sources, live_count):
    breadth, panel_rows = grads.shape
    block_size = values.shape[-1]
    row_blocks = panel_rows // block_size
    tiles = grads.reshape(breadth, row_blocks, block_size)
    slot_index = jnp.arange(values.shape[2], dtype=jnp.int32)

    def term_one_panel(source_panel):
        chosen = jnp.take(tiles, targets[0, source_panel], axis=1)
        product = jnp.einsum(
            "fsi,sij->fsj", chosen, values[0, source_panel], preferred_element_type=jnp.float32
        )
        live_slots = (slot_index < live_count[0, source_panel]).astype(jnp.float32)
        placed = jnp.zeros((breadth, row_blocks, block_size), jnp.float32)
        placed = placed.at[:, sources[0, source_panel]].add(product * live_slots[None, :, None])
        return placed.reshape(breadth, panel_rows)

    summed = lax.psum_scatter(
        lax.map(term_one_panel, jnp.arange(lax.axis_size("blk") * 1, dtype=jnp.int32)).astype(
            jnp.bfloat16
        ),
        "blk",
        scatter_dimension=0,
        tiled=True,
    ).astype(jnp.float32)
    return summed[0]


def mix_features(weight, table):
    out_part = weight.shape[1] // lax.axis_size("feat")
    position = lax.axis_index("feat")
    own_columns = lax.dynamic_slice_in_dim(weight, position * out_part, out_part, 1)
    return lax.dot_general(
        own_columns,
        lax.all_gather(table, "feat", axis=0, tiled=True),
        (((0,), (0,)), ((), ())),
        preferred_element_type=jnp.float32,
    )


def class_scores(weight_out, table):
    return lax.dot_general(
        weight_out,
        lax.all_gather(table, "feat", axis=0, tiled=True),
        (((0,), (0,)), ((), ())),
        preferred_element_type=jnp.float32,
    )


def weight_columns(gated, own_table, own_weight):
    breadth, panel_rows = own_table.shape
    total_out = gated.shape[0] * lax.axis_size("feat")

    def add_columns(running, portion):
        grad_part = running[0]
        product = lax.dot_general(
            own_table, portion, (((1,), (1,)), ((), ())), preferred_element_type=jnp.float32
        )
        grad_part = product
        if len(running) == 1:
            return (grad_part,)
        return (grad_part, jnp.dot(own_weight, portion, preferred_element_type=jnp.float32))

    grad_zero = jnp.zeros((breadth, total_out), jnp.float32)
    if own_weight is None:
        initial = (grad_zero,)
    else:
        initial = (grad_zero, jnp.zeros((own_weight.shape[0], panel_rows), jnp.float32))
    return add_columns(initial, lax.all_gather(gated, "feat", axis=0, tiled=True))


def shards(
    features,
    weight_in,
    weight_mid,
    weight_out,
    block_values,
    block_dst,
    block_src,
    block_count,
    labels,
    train_mask,
):
    position = lax.axis_index("feat")
    hidden_part = weight_mid.shape[0] // lax.axis_size("feat")
    block_size = block_values.shape[-1]
    in_part, panel_rows = features.shape
    row_blocks = panel_rows // block_size
    folding = panel_folder(
        block_values, block_dst, block_src, block_count, in_part, row_blocks, block_size
    )
    initial = jnp.zeros((in_part, row_blocks, block_size), jnp.float32)
    first_sum = folding(initial, lax.all_gather(features, "blk", axis=1, tiled=True), jnp.int32(0))
    first_agg = first_sum.reshape(in_part, panel_rows).astype(jnp.bfloat16)
    first_pre = mix_features(weight_in, first_agg)
    first_act = elu(first_pre).astype(jnp.bfloat16)
    second_agg = hidden_aggregate(first_act, block_values, block_dst, block_src, block_count)
    second_pre = mix_features(weight_mid, second_agg)
    second_act = elu(second_pre).astype(jnp.bfloat16)
    third_agg = hidden_aggregate(second_act, block_values, block_dst, block_src, block_count)
    out_rows = lax.dynamic_slice_in_dim(weight_out, position * hidden_part, hidden_part, 0)
    logits = class_scores(weight_out, third_agg)
    log_total = jnp.log(jnp.sum(jnp.exp(logits), axis=0))
    one_hot = (jnp.arange(logits.shape[0], dtype=jnp.int32)[:, None] == labels[None, :]).astype(
        jnp.float32
    )
    picked = jnp.sum(one_hot * logits, axis=0)
    weighting = train_mask.astype(jnp.float32)
    loss_total, node_count = lax.psum(
        (jnp.sum(weighting * (log_total - picked)), jnp.sum(weighting)), "blk"
    )
    loss = loss_total / jnp.maximum(node_count, 1.0)
    grad_logits = (weighting[None, :] * (jnp.exp(logits - log_total[None, :]) - one_hot)).astype(
        jnp.bfloat16
    )
    grad_out = lax.dot_general(
        third_agg, grad_logits, (((1,), (1,)), ((), ())), preferred_element_type=jnp.float32
    )
    grad_out = lax.psum(grad_out, "blk")
    third_back = jnp.dot(out_rows, grad_logits, preferred_element_type=jnp.float32).astype(
        jnp.bfloat16
    )
    second_grad = spread_back(third_back, block_values, block_dst, block_src, block_count)
    second_gate = (second_grad * elu_slope(second_pre)).astype(jnp.bfloat16)
    mid_rows = lax.dynamic_slice_in_dim(weight_mid, position * hidden_part, hidden_part, 0)
    grad_mid, second_back = weight_columns(second_gate, second_agg, mid_rows)
    grad_mid = lax.psum(grad_mid, "blk")
    first_grad = spread_back(
        second_back.astype(jnp.bfloat16), block_values, block_dst, block_src, block_count
    )
    first_gate = (first_grad * elu_slope(first_pre)).astype(jnp.bfloat16)
    grad_in = weight_columns(first_gate, first_agg, None)[0]
    grad_in = lax.psum(grad_in, "blk")
    grad_in, grad_mid, grad_out = (grad_in, grad_mid, grad_out)
    return (loss, grad_in, grad_mid, grad_out)


def solution(mesh):
    placed = (
        P("feat", "blk"),
        P(),
        P(),
        P(),
        P("blk", None, None, None, None),
        P("blk", None, None),
        P("blk", None, None),
        P("blk", None),
        P("blk"),
        P("blk"),
    )
    return jax.shard_map(
        shards,
        mesh=mesh,
        in_specs=placed,
        out_specs=(P(), P("feat", None), P("feat", None), P("feat", None)),
        check_vma=False,
    )
```

profile of v0, /device:TPU:0, one launch (start us, length us, event | category | flops | bytes accessed | tf_op | source)
XLA Modules:
  0.0 608.6 jit_solution(1737324306972229232)
XLA Ops:
  7.2 11.6 %all_gather.24 = bf16[32,8192]{1,0:T(8,128)(2,1)S(1)} all-gather(bf16[32,1024]{1,0:T(8,128)(2,1)} %param.22), channel_id=1, replica_groups=mesh['blk'=8,'feat'=4] {'blk'}, dimensions={1}, use_global_device_ids=true | all-gather | bytes 589824 | tf_op jit(solution)/shard_map/all_gather | solution.py:141
  18.9 53.0 %while.64 = (s32[]{:T(128)}, f32[32,8,128]{2,0,1:T(8,128)S(1)}, s32[1,8,16]{2,1,0:T(8,128)}, bf16[1,8,16,128,128]{4,3,2,1,0:T(8,128)(2,1)}, s32[1,8,16]{2,1,0:T(...) while((s32[]{:T(128)}, f32[32,8,128]{2,0,1:T(8,128)S(1)}, ...), condition=%wide.region_2.3_spmd.clone, body=%wide.region_0.2_spmd.clone.sunk | while | flops 16975076 | bytes 2102115 | solution.py:34
  22.8 1.5 fusion.121
  29.4 1.5 fusion.121
  36.1 1.5 fusion.121
  42.7 1.5 fusion.121
  49.3 1.5 fusion.121
  55.9 1.5 fusion.121
  71.9 14.1 %all_gather.25 = bf16[128,1024]{1,0:T(8,128)(2,1)S(1)} all-gather(bf16[32,1024]{1,0:T(8,128)(2,1)S(1)} %copy_bitcast_fusion.7), channel_id=1, replica_groups=mesh['blk'=8,'feat'=4] {'feat'}, dimensions={0}, use_global_device_ids=true | all-gather | bytes 327680 | tf_op jit(solution)/shard_map/all_gather | solution.py:83
  87.0 24.1 %all-gather.3.cloned.1.call-done = bf16[64,8192]{1,0:T(8,128)(2,1)} async-done(((bf16[64,1024]{1,0:T(8,128)(2,1)}), bf16[64,8192]{1,0:T(8,128)(2,1)}) %all-gather.3.cloned.1.call-update) | async-done | bytes 1048592 | tf_op jit(solution)/shard_map/all_gather | solution.py:45
  111.2 62.0 %while.65 = (s32[]{:T(128)}, f32[64,8,128]{2,0,1:T(8,128)S(1)}, s32[1,8,16]{2,1,0:T(8,128)}, bf16[1,8,16,128,128]{4,3,2,1,0:T(8,128)(2,1)}, bf16[64,8192]{1,0:T(...) while((s32[]{:T(128)}, f32[64,8,128]{2,0,1:T(8,128)S(1)}, ...), condition=%wide.region_5.7_spmd.clone, body=%wide.region_3.0_spmd.clone.sunk | while | flops 33948852 | bytes 3674915 | solution.py:34
  116.1 1.5 fusion.125
  123.8 1.5 fusion.125
  131.6 1.5 fusion.125
  139.3 1.5 fusion.125
  147.1 1.5 fusion.125
  154.8 1.5 fusion.125
  162.6 1.5 fusion.125
  170.3 1.5 fusion.125
  173.2 16.0 %all_gather.27 = bf16[256,1024]{1,0:T(8,128)(2,1)S(1)} all-gather(bf16[64,1024]{1,0:T(8,128)(2,1)S(1)} %copy_bitcast_fusion.4), channel_id=1, replica_groups=mesh['blk'=8,'feat'=4] {'feat'}, dimensions={0}, use_global_device_ids=true | all-gather | bytes 655360 | tf_op jit(solution)/shard_map/all_gather | solution.py:83
  190.3 24.0 %all-gather.5.cloned.1.call-done = bf16[64,8192]{1,0:T(8,128)(2,1)} async-done(((bf16[64,1024]{1,0:T(8,128)(2,1)}), bf16[64,8192]{1,0:T(8,128)(2,1)}) %all-gather.5.cloned.1.call-update) | async-done | bytes 1048592 | tf_op jit(solution)/shard_map/all_gather | solution.py:45
  214.3 62.0 %while.66 = (s32[]{:T(128)}, f32[64,8,128]{2,0,1:T(8,128)S(1)}, s32[1,8,16]{2,1,0:T(8,128)}, bf16[1,8,16,128,128]{4,3,2,1,0:T(8,128)(2,1)}, bf16[64,8192]{1,0:T(...) while((s32[]{:T(128)}, f32[64,8,128]{2,0,1:T(8,128)S(1)}, ...), condition=%wide.region_8.10_spmd.clone, body=%wide.region_6.9_spmd.clone.sunk | while | flops 33948852 | bytes 3674915 | solution.py:34
  219.2 1.5 fusion.129
  227.0 1.5 fusion.129
  234.7 1.5 fusion.129
  242.4 1.5 fusion.129
  250.2 1.5 fusion.129
  257.9 1.5 fusion.129
  265.7 1.5 fusion.129
  273.4 1.5 fusion.129
  276.4 16.0 %all_gather.29 = bf16[256,1024]{1,0:T(8,128)(2,1)S(1)} all-gather(bf16[64,1024]{1,0:T(8,128)(2,1)S(1)} %copy_bitcast_fusion.3), channel_id=1, replica_groups=mesh['blk'=8,'feat'=4] {'feat'}, dimensions={0}, use_global_device_ids=true | all-gather | bytes 655360 | tf_op jit(solution)/shard_map/all_gather | solution.py:92
  294.1 75.5 %while.67 = (s32[]{:T(128)}, bf16[8,64,1024]{2,1,0:T(8,128)(2,1)S(1)}, s32[8]{0:T(128)S(1)}, s32[1,8,16]{2,1,0:T(8,128)}, bf16[1,8,16,128,128]{4,3,2,1,0:T(8,128...) while((s32[]{:T(128)}, ...), condition=%wide.region_17.19_spmd.clone, body=%wide.region_15.18_spmd.clone.sunk | while | flops 33948852 | bytes 4592431 | solution.py:67
  370.7 36.5 %reduce-scatter.3.cloned.1.call-done = bf16[1,64,1024]{2,1,0:T(8,128)(2,1)} async-done(((bf16[8,64,1024]{2,1,0:T(8,128)(2,1)}), bf16[1,64,1024]{2,1,0:T(8,128)(2,1)}) %reduce-scatter.3.cloned.1.call-update) | async-done | bytes 131088 | tf_op jit(solution)/shard_map/reduce_scatter | solution.py:66
  408.2 15.4 %all_gather.30 = bf16[256,1024]{1,0:T(8,128)(2,1)S(1)} all-gather(bf16[64,1024]{1,0:T(8,128)(2,1)S(1)} %fusion.75), channel_id=1, replica_groups=mesh['blk'=8,'feat'=4] {'feat'}, dimensions={0}, use_global_device_ids=true | all-gather | bytes 655360 | tf_op jit(solution)/shard_map/all_gather | solution.py:117
  424.0 80.9 %while.68 = (s32[]{:T(128)}, bf16[8,64,1024]{2,1,0:T(8,128)(2,1)S(1)}, s32[8]{0:T(128)S(1)}, s32[1,8,16]{2,1,0:T(8,128)}, bf16[1,8,16,128,128]{4,3,2,1,0:T(8,128...) while((s32[]{:T(128)}, ...), condition=%wide.region_21.23_spmd.clone, body=%wide.region_19.22_spmd.clone.sunk | while | flops 33948852 | bytes 4592743 | solution.py:67
  432.3 1.5 scatter_fusion.4
  442.4 1.5 scatter_fusion.4
  452.5 1.5 scatter_fusion.4
  462.7 1.5 scatter_fusion.4
  472.8 1.5 scatter_fusion.4
  482.9 1.5 scatter_fusion.4
  493.0 1.5 scatter_fusion.4
  503.1 1.5 scatter_fusion.4
  508.3 34.5 %reduce-scatter.5.cloned.1.call-done = bf16[1,64,1024]{2,1,0:T(8,128)(2,1)} async-done(((bf16[8,64,1024]{2,1,0:T(8,128)(2,1)}), bf16[1,64,1024]{2,1,0:T(8,128)(2,1)}) %reduce-scatter.5.cloned.1.call-update) | async-done | bytes 131088 | tf_op jit(solution)/shard_map/reduce_scatter | solution.py:66
  543.7 15.4 %all_gather.31 = bf16[256,1024]{1,0:T(8,128)(2,1)S(1)} all-gather(bf16[64,1024]{1,0:T(8,128)(2,1)S(1)} %fusion.73), channel_id=1, replica_groups=mesh['blk'=8,'feat'=4] {'feat'}, dimensions={0}, use_global_device_ids=true | all-gather | bytes 655360 | tf_op jit(solution)/shard_map/all_gather | solution.py:117
  559.4 24.2 %all-reduce.5 = (f32[]{:T(128)}, f32[]{:T(128)}, f32[32,256]{1,0:T(8,128)}, f32[64,172]{1,0:T(8,128)}) all-reduce(f32[]{:T(128)} %get-tuple-element.640, f32[]{:T(128)} %get-tuple-element.639, f32[32,256]{1,0:T(8,128)S(1)} %fusion.88, f32[64,172]{1,0:T(8,128)S(1)} %fusion.90), channel_id=1, replica_groups=mesh['blk'=8,'feat'=4] {'blk'}, use_global_device_ids=true, to_apply=%region_12.14 | all-reduce | flops 19202 | bytes 153616 | tf_op jit(solution)/shard_map/psum | solution.py:157
  584.8 14.6 %all-reduce.4.cloned.1.call-done = f32[64,256]{1,0:T(8,128)} async-done(((f32[64,256]{1,0:T(8,128)}), f32[64,256]{1,0:T(8,128)}) %all-reduce.4.cloned.1.call-update) | async-done | bytes 65552 | tf_op jit(solution)/shard_map/psum | solution.py:175
  599.4 1.5 copy.108
  (436 shorter events, 265.5 us)
Async XLA Ops:
  7.2 182.1 %copy-start = (bf16[256,256]{1,0:T(8,128)(2,1)S(1)}, bf16[256,256]{1,0:T(8,128)(2,1)}, u32[]{:S(2)}) copy-start(bf16[256,256]{1,0:T(8,128)(2,1)} %param.24) | copy-start | bytes 393220
  7.2 104.0 %all-gather.3.cloned.1.call-start = ((), (), s32[]{:S(2)}) async-start(), calls=%async_computation.2 | async-start | bytes 1179648 | tf_op jit(solution)/shard_map/all_gather | solution.py:45
  18.9 67.1 %copy-start.6 = (bf16[128,256]{1,0:T(8,128)(2,1)S(1)}, bf16[128,256]{1,0:T(8,128)(2,1)}, u32[]{:S(2)}) copy-start(bf16[128,256]{1,0:T(8,128)(2,1)} %param.23) | copy-start | bytes 196612
  87.0 127.3 %all-gather.5.cloned.1.call-start = ((), (), s32[]{:S(2)}) async-start(), calls=%async_computation.3 | async-start | bytes 1179648 | tf_op jit(solution)/shard_map/all_gather | solution.py:45
  111.2 79.1 %copy-start.7 = (s32[1024]{0:T(1024)S(1)}, s32[1024]{0:T(1024)}, u32[]{:S(2)}) copy-start(s32[1024]{0:T(1024)} %param.31) | copy-start | bytes 12292
  190.3 217.0 %reduce-scatter.3.cloned.1.call-start = ((), (), s32[]{:S(2)}) async-start(), calls=%async_computation.4 | async-start | bytes 1179648 | tf_op jit(solution)/shard_map/reduce_scatter | solution.py:66
  214.3 78.1 %copy-start.4 = (bf16[256,172]{0,1:T(8,128)(2,1)S(1)}, bf16[256,172]{0,1:T(8,128)(2,1)}, u32[]{:S(2)}) copy-start(bf16[256,172]{0,1:T(8,128)(2,1)} %param.25) | copy-start | bytes 264196
  214.3 78.1 %copy-start.5 = (s32[1024]{0:T(1024)S(1)}, s32[1024]{0:T(1024)}, u32[]{:S(2)}) copy-start(s32[1024]{0:T(1024)} %param.30) | copy-start | bytes 12292
  292.7 1.2 copy-start.3
  369.6 1.0 copy-start.1
  370.6 172.1 %reduce-scatter.5.cloned.1.call-start = ((), (), s32[]{:S(2)}) async-start(), calls=%async_computation.5 | async-start | bytes 1179648 | tf_op jit(solution)/shard_map/reduce_scatter | solution.py:66
  424.0 3.8 copy-start.8
  432.3 1.8 copy-start.9
  434.1 3.8 copy-start.8
  442.4 1.8 copy-start.9
  444.2 3.8 copy-start.8
  452.5 1.8 copy-start.9
  454.3 3.8 copy-start.8
  462.6 1.8 copy-start.9
  464.4 3.8 copy-start.8
  472.7 1.8 copy-start.9
  474.5 3.8 copy-start.8
  482.8 1.8 copy-start.9
  484.6 3.8 copy-start.8
  492.9 1.8 copy-start.9
  494.7 3.8 copy-start.8
  503.1 1.8 copy-start.9
  504.8 1.0 copy-start.2
  505.8 93.6 %all-reduce.4.cloned.1.call-start = ((), (), s32[]{:S(2)}) async-start(), calls=%async_computation.6 | async-start | bytes 131072 | tf_op jit(solution)/shard_map/psum | solution.py:175
Sparse Core Ops, SparseCore 0:
  87.1 24.0 all-gather.2
  190.4 23.8 all-gather.4
  370.8 36.4 reduce-scatter.2
  506.0 36.7 reduce-scatter.4
  546.2 53.1 all-reduce.3
where the time goes:
time: 615 us; the launch traced here: 609 us
  other arithmetic  142 us (23%)
  waiting for transfers between devices  134 us (22%)
  blocking collectives  113 us (18%)
  local copies, waits for them, and re-layouts  106 us (17%)
  matrix products  63.7 us (10%)
  loops' own time  33.6 us (5%)
  between operations  16.4 us (3%)
    reduce_scatter x2, waiting for transfers between devices, spread_back(): lax.psum_scatter(lax.map(term_one_panel, jnp.arange(lax.axis_size('blk')...  71 us
    all_gather x2, waiting for transfers between devices, hidden_aggregate(): lax.all_gather(table, 'blk', axis=1, tiled=True)  48.1 us
    dot_general x24, matrix products, folding_one_panel(): jnp.einsum('fsj,sij->fsi', chosen, values[0, turn_index], preferred_eleme...  36.4 us
    another operation x2, loops' own time, spread_back(): lax.map(term_one_panel, jnp.arange(lax.axis_size('blk') * 1, dtype=jnp.in...  32.5 us
    scatter-add x24, other arithmetic, folding_one_panel(): accumulated.at[:, targets[0, turn_index]]  31.2 us
    all_gather x2, blocking collectives, weight_columns(): lax.all_gather(gated, 'feat', axis=0, tiled=True)  30.8 us
    all_gather x2, blocking collectives, mix_features(): lax.all_gather(table, 'feat', axis=0, tiled=True)  30.1 us
    dynamic_slice x24, local copies, waits for them, and re-layouts, folding_one_panel(): live_slots = (slot_index < live_count[0, turn_index]).astype(jnp.float32)  29.8 us
  transfers between devices with their start and end apart: 5, of which 5 were waited for; matrix products, arithmetic and copies ran while one was open for 1% of the time, Pallas kernels for 0%

commit v1 on v0

--- a/solution.py
+++ b/solution.py
@@ -2,6 +2,7 @@
 import jax.numpy as jnp
 from jax import lax
 from jax.sharding import PartitionSpec as P
+from jax.lax import axis_index, axis_size, ppermute
 
 
 def elu(values):
@@ -42,7 +43,31 @@
     row_blocks = panel_rows // block_size
     folding = panel_folder(values, targets, sources, live_count, breadth, row_blocks, block_size)
     initial = jnp.zeros((breadth, row_blocks, block_size), jnp.float32)
-    summed = folding(initial, lax.all_gather(table, "blk", axis=1, tiled=True), jnp.int32(0))
+
+    def slabs_place(xx):
+        g_now = axis_index("blk")
+        m_next = axis_size("blk")
+        tmp, part_now, v_next = (m_next, g_now, xx.shape[1])
+        queue = list(map(lambda at: (at, (at + 1) % tmp), range(tmp)))
+        local_out = range(tmp)
+        line_up = list(map(lambda at: (at, (at - 1) % tmp), local_out))
+        mixed_arr = jnp.zeros((*xx.shape[:1], tmp * v_next, *xx.shape[2:]), xx.dtype)
+        taken_in = d_next = xx
+        block_last = tmp // 2
+        mixed_arr = lax.dynamic_update_slice_in_dim(mixed_arr, xx, part_now * v_next, axis=1)
+        for j in range(1, block_last + 1):
+            taken_in = ppermute(taken_in, axis_name="blk", perm=queue)
+            mixed_arr = lax.dynamic_update_slice_in_dim(
+                mixed_arr, taken_in, (part_now - j) % tmp * v_next, axis=1
+            )
+            if j < tmp - block_last:
+                d_next = ppermute(d_next, axis_name="blk", perm=line_up)
+                mixed_arr = lax.dynamic_update_slice_in_dim(
+                    mixed_arr, d_next, (part_now + j) % tmp * v_next, axis=1
+                )
+        return mixed_arr
+
+    summed = folding(initial, slabs_place(table), jnp.int32(0))
     return summed.reshape(breadth, panel_rows).astype(jnp.bfloat16)
 
 

time: 615 us -> 595 us (0.967)
  waiting for transfers between devices: 134 us -> 113 us
  starting transfers between devices: 0.2 us -> 16.2 us
  local copies, waits for them, and re-layouts: 106 us -> 97.3 us
    all_gather x2 -> x0, waiting for transfers between devices: 48.1 us -> none  [hidden_aggregate(): lax.all_gather(table, 'blk', axis=1, tiled=True)]
    ppermute x0 -> x14, waiting for transfers between devices: none -> 28.8 us  [the longest x8 28.8 us: slabs_place(): taken_in = ppermute(taken_in, axis_name='blk', perm=queue)]
    ppermute x0 -> x14, starting transfers between devices: none -> 16.1 us  [the longest x6 15.9 us: slabs_place(): d_next = ppermute(d_next, axis_name='blk', perm=line_up)]
    reshape x24, local copies, waits for them, and re-layouts: 15.1 us -> 0.63 us  [folding_one_panel(): window = window.reshape(breadth, row_blocks, block_size)]
  transfers between devices with their start and end apart: 5 -> 17, of which waited for: 5 -> 11; matrix products, arithmetic and copies ran while one was open for 1% -> 1% of each run, Pallas kernels for 0% -> 0%
where the time goes in v1:
time: 595 us; the launch traced here: 589 us
  other arithmetic  137 us (23%)
  blocking collectives  113 us (19%)
  waiting for transfers between devices  113 us (19%)
  local copies, waits for them, and re-layouts  97.3 us (16%)
  matrix products  62.4 us (10%)
  loops' own time  33.4 us (6%)
  between operations  16.6 us (3%)
  starting transfers between devices  16.2 us (3%)
    reduce_scatter x2, waiting for transfers between devices, spread_back(): lax.psum_scatter(lax.map(term_one_panel, jnp.arange(lax.axis_size('blk')...  69.4 us
    dot_general x24, matrix products, folding_one_panel(): jnp.einsum('fsj,sij->fsi', chosen, values[0, turn_index], preferred_eleme...  36.3 us
    another operation x2, loops' own time, spread_back(): lax.map(term_one_panel, jnp.arange(lax.axis_size('blk') * 1, dtype=jnp.in...  32.2 us
    scatter-add x24, other arithmetic, folding_one_panel(): accumulated.at[:, targets[0, turn_index]]  31.2 us
    all_gather x2, blocking collectives, weight_columns(): lax.all_gather(gated, 'feat', axis=0, tiled=True)  30.7 us
    all_gather x2, blocking collectives, mix_features(): lax.all_gather(table, 'feat', axis=0, tiled=True)  30.2 us
    dynamic_slice x24, local copies, waits for them, and re-layouts, folding_one_panel(): live_slots = (slot_index < live_count[0, turn_index]).astype(jnp.float32)  29.8 us
    ppermute x8, waiting for transfers between devices, slabs_place(): taken_in = ppermute(taken_in, axis_name='blk', perm=queue)  28.8 us
  transfers between devices with their start and end apart: 17, of which 11 were waited for; matrix products, arithmetic and copies ran while one was open for 1% of the time, Pallas kernels for 0%

profile of v1, /device:TPU:0, one launch (start us, length us, event | category | flops | bytes accessed | tf_op | source)
XLA Modules:
  0.0 588.9 jit_solution(5558316345303115906)
XLA Ops:
  7.2 11.6 %all_gather.18 = bf16[32,8192]{1,0:T(8,128)(2,1)S(1)} all-gather(bf16[32,1024]{1,0:T(8,128)(2,1)} %param.22), channel_id=1, replica_groups=mesh['blk'=8,'feat'=4] {'blk'}, dimensions={1}, use_global_device_ids=true | all-gather | bytes 589824 | tf_op jit(solution)/shard_map/all_gather | solution.py:166
  18.9 52.9 %while.64 = (s32[]{:T(128)}, f32[32,8,128]{2,0,1:T(8,128)S(1)}, s32[1,8,16]{2,1,0:T(8,128)}, bf16[1,8,16,128,128]{4,3,2,1,0:T(8,128)(2,1)}, s32[1,8,16]{2,1,0:T(...) while((s32[]{:T(128)}, f32[32,8,128]{2,0,1:T(8,128)S(1)}, ...), condition=%wide.region_2.3_spmd.clone, body=%wide.region_0.2_spmd.clone.sunk | while | flops 16975076 | bytes 2102615 | solution.py:35
  22.8 1.5 fusion.123
  29.4 1.5 fusion.123
  71.9 14.1 %all_gather.19 = bf16[128,1024]{1,0:T(8,128)(2,1)S(1)} all-gather(bf16[32,1024]{1,0:T(8,128)(2,1)S(1)} %copy_bitcast_fusion.7), channel_id=1, replica_groups=mesh['blk'=8,'feat'=4] {'feat'}, dimensions={0}, use_global_device_ids=true | all-gather | bytes 327680 | tf_op jit(solution)/shard_map/all_gather | solution.py:108
  86.5 2.6 collective-permute-start.1
  89.1 3.2 collective-permute-done
  92.3 2.6 collective-permute-start.3
  95.0 4.0 collective-permute-done.2
  98.9 2.6 collective-permute-start.5
  101.6 3.5 collective-permute-done.4
  105.1 5.2 collective-permute-done.6
  110.4 54.8 %while.65 = (s32[]{:T(128)}, f32[64,8,128]{2,0,1:T(8,128)S(1)}, s32[1,8,16]{2,1,0:T(8,128)}, bf16[1,8,16,128,128]{4,3,2,1,0:T(8,128)(2,1)}, bf16[64,8192]{1,0:T(...) while((s32[]{:T(128)}, f32[64,8,128]{2,0,1:T(8,128)S(1)}, ...), condition=%wide.region_5.7_spmd.clone, body=%wide.region_3.0_spmd.clone.sunk | while | flops 33948852 | bytes 3675415 | solution.py:35
  113.7 1.5 fusion.127
  120.5 1.5 fusion.127
  127.4 1.5 fusion.127
  134.2 1.5 fusion.127
  141.1 1.5 fusion.127
  147.9 1.5 fusion.127
  154.8 1.5 fusion.127
  161.6 1.5 fusion.127
  165.3 16.1 %all_gather.20 = bf16[256,1024]{1,0:T(8,128)(2,1)S(1)} all-gather(bf16[64,1024]{1,0:T(8,128)(2,1)S(1)} %copy_bitcast_fusion.4), channel_id=1, replica_groups=mesh['blk'=8,'feat'=4] {'feat'}, dimensions={0}, use_global_device_ids=true | all-gather | bytes 655360 | tf_op jit(solution)/shard_map/all_gather | solution.py:108
  181.9 2.6 collective-permute-start.8
  184.5 2.6 collective-permute-done.7
  187.2 2.7 collective-permute-start.10
  189.9 2.6 collective-permute-done.9
  192.5 2.7 collective-permute-start.12
  195.2 2.6 collective-permute-done.11
  197.8 5.2 collective-permute-done.13
  203.1 54.8 %while.66 = (s32[]{:T(128)}, f32[64,8,128]{2,0,1:T(8,128)S(1)}, s32[1,8,16]{2,1,0:T(8,128)}, bf16[1,8,16,128,128]{4,3,2,1,0:T(8,128)(2,1)}, bf16[64,8192]{1,0:T(...) while((s32[]{:T(128)}, f32[64,8,128]{2,0,1:T(8,128)S(1)}, ...), condition=%wide.region_8.10_spmd.clone, body=%wide.region_6.9_spmd.clone.sunk | while | flops 33948852 | bytes 3675415 | solution.py:35
  206.3 1.5 fusion.131
  213.2 1.5 fusion.131
  220.0 1.5 fusion.131
  226.9 1.5 fusion.131
  233.8 1.5 fusion.131
  240.6 1.5 fusion.131
  247.5 1.5 fusion.131
  254.3 1.5 fusion.131
  257.9 15.9 %all_gather.21 = bf16[256,1024]{1,0:T(8,128)(2,1)S(1)} all-gather(bf16[64,1024]{1,0:T(8,128)(2,1)S(1)} %copy_bitcast_fusion.3), channel_id=1, replica_groups=mesh['blk'=8,'feat'=4] {'feat'}, dimensions={0}, use_global_device_ids=true | all-gather | bytes 655360 | tf_op jit(solution)/shard_map/all_gather | solution.py:117
  275.4 75.5 %while.67 = (s32[]{:T(128)}, bf16[8,64,1024]{2,1,0:T(8,128)(2,1)S(1)}, s32[8]{0:T(128)S(1)}, s32[1,8,16]{2,1,0:T(8,128)}, bf16[1,8,16,128,128]{4,3,2,1,0:T(8,128...) while((s32[]{:T(128)}, ...), condition=%wide.region_17.19_spmd.clone, body=%wide.region_15.18_spmd.clone.sunk | while | flops 33948852 | bytes 4592423 | solution.py:92
  352.0 34.9 %reduce-scatter.3.cloned.1.call-done = bf16[1,64,1024]{2,1,0:T(8,128)(2,1)} async-done(((bf16[8,64,1024]{2,1,0:T(8,128)(2,1)}), bf16[1,64,1024]{2,1,0:T(8,128)(2,1)}) %reduce-scatter.3.cloned.1.call-update) | async-done | bytes 131088 | tf_op jit(solution)/shard_map/reduce_scatter | solution.py:91
  387.9 15.4 %all_gather.22 = bf16[256,1024]{1,0:T(8,128)(2,1)S(1)} all-gather(bf16[64,1024]{1,0:T(8,128)(2,1)S(1)} %fusion.75), channel_id=1, replica_groups=mesh['blk'=8,'feat'=4] {'feat'}, dimensions={0}, use_global_device_ids=true | all-gather | bytes 655360 | tf_op jit(solution)/shard_map/all_gather | solution.py:142
  404.2 80.8 %while.68 = (s32[]{:T(128)}, bf16[8,64,1024]{2,1,0:T(8,128)(2,1)S(1)}, s32[8]{0:T(128)}, s32[1,8,16]{2,1,0:T(8,128)}, bf16[1,8,16,128,128]{4,3,2,1,0:T(8,128)(2,...) while((s32[]{:T(128)}, ...), condition=%wide.region_21.23_spmd.clone, body=%wide.region_19.22_spmd.clone.sunk | while | flops 33948852 | bytes 4592423 | solution.py:92
  488.4 34.5 %reduce-scatter.5.cloned.1.call-done = bf16[1,64,1024]{2,1,0:T(8,128)(2,1)} async-done(((bf16[8,64,1024]{2,1,0:T(8,128)(2,1)}), bf16[1,64,1024]{2,1,0:T(8,128)(2,1)}) %reduce-scatter.5.cloned.1.call-update) | async-done | bytes 131088 | tf_op jit(solution)/shard_map/reduce_scatter | solution.py:91
  523.9 15.4 %all_gather.23 = bf16[256,1024]{1,0:T(8,128)(2,1)S(1)} all-gather(bf16[64,1024]{1,0:T(8,128)(2,1)S(1)} %fusion.73), channel_id=1, replica_groups=mesh['blk'=8,'feat'=4] {'feat'}, dimensions={0}, use_global_device_ids=true | all-gather | bytes 655360 | tf_op jit(solution)/shard_map/all_gather | solution.py:142
  539.5 24.1 %all-reduce.5 = (f32[]{:T(128)}, f32[]{:T(128)}, f32[32,256]{1,0:T(8,128)}, f32[64,172]{1,0:T(8,128)}) all-reduce(f32[]{:T(128)} %get-tuple-element.640, f32[]{:T(128)} %get-tuple-element.639, f32[32,256]{1,0:T(8,128)S(1)} %fusion.88, f32[64,172]{1,0:T(8,128)S(1)} %fusion.90), channel_id=1, replica_groups=mesh['blk'=8,'feat'=4] {'blk'}, use_global_device_ids=true, to_apply=%region_12.14 | all-reduce | flops 19202 | bytes 153616 | tf_op jit(solution)/shard_map/psum | solution.py:182
  565.0 14.8 %all-reduce.4.cloned.1.call-done = f32[64,256]{1,0:T(8,128)} async-done(((f32[64,256]{1,0:T(8,128)}), f32[64,256]{1,0:T(8,128)}) %all-reduce.4.cloned.1.call-update) | async-done | bytes 65552 | tf_op jit(solution)/shard_map/psum | solution.py:200
  579.8 1.5 copy.124
  (442 shorter events, 268.3 us)
Async XLA Ops:
  7.2 174.3 %copy-start = (bf16[256,256]{1,0:T(8,128)(2,1)S(1)}, bf16[256,256]{1,0:T(8,128)(2,1)}, u32[]{:S(2)}) copy-start(bf16[256,256]{1,0:T(8,128)(2,1)} %param.24) | copy-start | bytes 393220
  7.2 379.8 %reduce-scatter.3.cloned.1.call-start = ((), (), s32[]{:S(2)}) async-start(), calls=%async_computation.2 | async-start | bytes 1179648 | tf_op jit(solution)/shard_map/reduce_scatter | solution.py:91
  18.9 67.2 %copy-start.6 = (bf16[128,256]{1,0:T(8,128)(2,1)S(1)}, bf16[128,256]{1,0:T(8,128)(2,1)}, u32[]{:S(2)}) copy-start(bf16[128,256]{1,0:T(8,128)(2,1)} %param.23) | copy-start | bytes 196612
  86.4 5.9 collective-permute-start
  86.5 5.8 collective-permute-start.1
  92.3 6.6 %collective-permute-start.2 = (bf16[64,1024]{1,0:T(8,128)(2,1)S(1)}, bf16[64,1024]{1,0:T(8,128)(2,1)S(1)}, u32[]{:S(2)}, u32[]{:S(2)}) collective-permute-start(bf16[64,1024]{1,0:T(8,128)(2,1)S(1)} %collective-permute-done), channel_id=1, source_target_pairs={{0,4},{4,8},{8,12},{12,16},{16,20},{20,24},{24,28},{28,0},{1,5},{5... | collective-permute-start | bytes 393224 | tf_op jit(solution)/shard_map/ppermute | solution.py:59
  92.3 6.6 %collective-permute-start.3 = (bf16[64,1024]{1,0:T(8,128)(2,1)S(1)}, bf16[64,1024]{1,0:T(8,128)(2,1)S(1)}, u32[]{:S(2)}, u32[]{:S(2)}) collective-permute-start(bf16[64,1024]{1,0:T(8,128)(2,1)S(1)} %collective-permute-done.1), channel_id=1, source_target_pairs={{0,28},{4,0},{8,4},{12,8},{16,12},{20,16},{24,20},{28,24},{1,29},{... | collective-permute-start | bytes 393224 | tf_op jit(solution)/shard_map/ppermute | solution.py:64
  98.9 6.1 %collective-permute-start.4 = (bf16[64,1024]{1,0:T(8,128)(2,1)S(1)}, bf16[64,1024]{1,0:T(8,128)(2,1)S(1)}, u32[]{:S(2)}, u32[]{:S(2)}) collective-permute-start(bf16[64,1024]{1,0:T(8,128)(2,1)S(1)} %collective-permute-done.2), channel_id=1, source_target_pairs={{0,4},{4,8},{8,12},{12,16},{16,20},{20,24},{24,28},{28,0},{1,5},{5... | collective-permute-start | bytes 393224 | tf_op jit(solution)/shard_map/ppermute | solution.py:59
  98.9 6.2 %collective-permute-start.5 = (bf16[64,1024]{1,0:T(8,128)(2,1)S(1)}, bf16[64,1024]{1,0:T(8,128)(2,1)S(1)}, u32[]{:S(2)}, u32[]{:S(2)}) collective-permute-start(bf16[64,1024]{1,0:T(8,128)(2,1)S(1)} %collective-permute-done.3), channel_id=1, source_target_pairs={{0,28},{4,0},{8,4},{12,8},{16,12},{20,16},{24,20},{28,24},{1,29},{... | collective-permute-start | bytes 393224 | tf_op jit(solution)/shard_map/ppermute | solution.py:64
  105.1 5.3 collective-permute-start.6
  110.4 74.1 %copy-start.7 = (s32[1024]{0:T(1024)S(1)}, s32[1024]{0:T(1024)}, u32[]{:S(2)}) copy-start(s32[1024]{0:T(1024)} %param.31) | copy-start | bytes 12292
  181.8 5.3 collective-permute-start.7
  181.9 5.3 collective-permute-start.8
  187.1 5.3 collective-permute-start.9
  187.2 5.3 collective-permute-start.10
  192.4 5.3 collective-permute-start.11
  192.5 5.3 collective-permute-start.12
  197.7 5.3 collective-permute-start.13
  203.1 70.8 %copy-start.4 = (bf16[256,172]{0,1:T(8,128)(2,1)S(1)}, bf16[256,172]{0,1:T(8,128)(2,1)}, u32[]{:S(2)}) copy-start(bf16[256,172]{0,1:T(8,128)(2,1)} %param.25) | copy-start | bytes 264196
  203.1 70.8 %copy-start.5 = (s32[1024]{0:T(1024)S(1)}, s32[1024]{0:T(1024)}, u32[]{:S(2)}) copy-start(s32[1024]{0:T(1024)} %param.30) | copy-start | bytes 12292
  274.2 1.1 copy-start.3
  351.0 1.0 copy-start.1
  352.0 170.9 %reduce-scatter.5.cloned.1.call-start = ((), (), s32[]{:S(2)}) async-start(), calls=%async_computation.3 | async-start | bytes 1179648 | tf_op jit(solution)/shard_map/reduce_scatter | solution.py:91
  485.0 1.0 copy-start.2
  486.0 93.8 %all-reduce.4.cloned.1.call-start = ((), (), s32[]{:S(2)}) async-start(), calls=%async_computation.4 | async-start | bytes 131072 | tf_op jit(solution)/shard_map/psum | solution.py:200
Sparse Core Ops, SparseCore 0:
  352.1 34.8 reduce-scatter.2
  486.1 36.7 reduce-scatter.4
  526.5 53.1 all-reduce.3
